TPU v7x, 128 devices: a whole 4x4x4 slice. The times are simulated.
128 devices in a mesh: ex: 16 (over x, z), ey: 8 (over y, core).
Axes of the slice: x: 4, y: 4, z: 4, core: 2. Of those that a mesh axis runs over, the one named last changes fastest.
Arguments:
- crm_state: float32 [5, 12, 32, 16384], P(None, None, None, ('ex', 'ey')), may hold values from -6 to 6
- gcm_state: float32 [5, 12, 64, 16, 4, 4], P(None, None, 'ex', 'ey'), may hold values from -6 to 6
- mass: float32 [12, 64, 16, 4, 4], P(None, 'ex', 'ey'), may hold values from 0.5 to 2
- dest: int32 [16384, 1], P(('ex', 'ey')), may hold values from 0 to 127; in each aligned block of 128 rows (0 to 127, 128 to 255, ...) at most 2 rows name the same one
- cost_class: int32 [16384], P(('ex', 'ey')), may hold values from 1 to 2
Outputs:
- cloud_slots: float32 [5, 12, 32, 32768], P(None, None, None, ('ex', 'ey'))
- gcm_out: float32 [5, 12, 64, 16, 4, 4], P(None, None, 'ex', 'ey')
Inputs may be any that keep to these rules, and one draw needn't show every extreme that they name: Among the 128 columns of one device's block, at most 2 have the same dest, and some block reaches 2.
All inputs are finite; a program needn't handle non-finite values.
Results may differ from a plain program's by a relative error of at most 0.00002.
Values sent between devices are 32-bit elements; how exact they have to be, the bound alone decides.
A program may use at most 128 MiB of HBM per device.

v0:
```python
import functools
import random

import jax
import jax.numpy as jnp
from jax import lax
from jax.experimental import pallas as pl
from jax.experimental.pallas import tpu as pltpu
from jax.sharding import PartitionSpec as P

MESH = pl.DeviceIdType.MESH
HIGHEST = lax.Precision.HIGHEST
FIELDS, LEVELS, WIDTH, OWNED, DEVICES = 5, 12, 32, 128, 128
N_EX, N_EY = 16, 8
HALO_ROWS = 80
HALOS = (
    (0, 8, -1, 0),
    (8, 8, 1, 0),
    (16, 16, 0, -1),
    (32, 16, 0, 1),
    (48, 8, -1, -1),
    (56, 8, -1, 1),
    (64, 8, 1, -1),
    (72, 8, 1, 1),
)


def far_first():
    steps = [
        (dx, dy, dz, dc)
        for dx in range(4)
        for dy in range(4)
        for dz in range(4)
        for dc in range(2)
    ][1:]
    random.Random(0).shuffle(steps)
    return sorted(steps, key=lambda s: -sum(min(v, 4 - v) for v in s[:3]))


STEPS = far_first()


def nt_dot(a, b, precision=None):
    return lax.dot_general(
        a, b, (((1,), (1,)), ((), ())), precision=precision, preferred_element_type=jnp.float32
    )


def tn_dot(a, b, precision=None):
    return lax.dot_general(
        a, b, (((0,), (0,)), ((), ())), precision=precision, preferred_element_type=jnp.float32
    )


def level_step(source, z, profiles):
    values = [source[f, z + 1] for f in range(FIELDS)]
    drift = 0.075 * values[0]
    condensed = 0.4 * jnp.maximum(values[3], 0.0)
    after = []
    for f in range(FIELDS):
        s = values[f]
        east = pltpu.roll(s, WIDTH - 1, 0)
        west = pltpu.roll(s, 1, 0)
        nudged = 0.5 * (profiles[pl.ds(f * LEVELS + z, 1), :] - jnp.mean(s, axis=0, keepdims=True))
        change = 0.1 * (east + west + source[f, z + 2] + source[f, z] - 4.0 * s)
        change = change - drift * (east - west) + nudged
        if f == 1:
            change = change + 0.3 * values[2]
        elif f == 2:
            change = change - 0.3 * values[1] + 0.5 * condensed
        elif f == 3:
            change = change - condensed
        elif f == 4:
            change = change + condensed - 0.2 * s
        after.append(s + change)
    return values, after


def cloud_kernel(
    crm, gcm, mass, dest, cost, landed, gcm_out,
    start, first, second, profiles, weighted, faces, halo, outgoing,
    load_sem, own_sem, send_sem, recv_sem, face_send, face_recv,
):
    ex, ey = lax.axis_index("ex"), lax.axis_index("ey")
    me = ex * N_EY + ey
    px, pz, py, pc = ex // 4, ex % 4, ey // 2, ey % 2

    def peer(step):
        dx, dy, dz, dc = step
        return (
            ((px + dx) % 4) * 4 + (pz + dz) % 4,
            ((py + dy) % 4) * 2 + (pc + dc) % 2,
        )

    load = pltpu.make_async_copy(crm, start.at[:, pl.ds(1, LEVELS)], load_sem)
    load.start()
    barrier = pltpu.get_barrier_semaphore()
    for step in STEPS:
        pl.semaphore_signal(barrier, inc=1, device_id=peer(step), device_id_type=MESH)

    row = lax.broadcasted_iota(jnp.int32, (OWNED, OWNED), 0)
    lane = lax.broadcasted_iota(jnp.int32, (OWNED, OWNED), 1)
    target = dest[...].astype(jnp.float32)
    target_rows = jnp.sum(jnp.where(row == lane, target, 0.0), axis=1, keepdims=True)
    earlier = jnp.where((target_rows == target) & (row < lane), 1.0, 0.0)
    slot = jnp.sum(earlier, axis=0, keepdims=True) * DEVICES + target
    slots = lax.broadcasted_iota(jnp.int32, (2 * DEVICES, OWNED), 0).astype(jnp.float32)
    chosen = jnp.where(slots == slot, 1.0, 0.0).astype(jnp.bfloat16)

    for f in range(FIELDS):
        profiles[f * LEVELS:(f + 1) * LEVELS, :] = jnp.swapaxes(gcm[f], 0, 1)
    mass_rows = jnp.swapaxes(mass[...], 0, 1)

    zero = jnp.zeros((WIDTH, OWNED), jnp.float32)
    for f in range(FIELDS):
        for z in (0, LEVELS + 1):
            start[f, z] = zero
            first[f, z] = zero
    load.wait()
    substeps = cost[...].astype(jnp.float32)
    once, twice = substeps >= 1.0, substeps >= 2.0

    @pl.loop(0, LEVELS)
    def _(z):
        values, after = level_step(start, z, profiles)
        for f in range(FIELDS):
            first[f, z + 1] = jnp.where(once, after[f], values[f])

    @pl.loop(0, LEVELS)
    def _(z):
        values, after = level_step(first, z, profiles)
        for f in range(FIELDS):
            updated = jnp.where(twice, after[f], values[f])
            second[f, z] = updated
            tendency = jnp.mean(updated - start[f, z + 1], axis=0, keepdims=True)
            weighted[pl.ds(f * LEVELS + z, 1), :] = tendency

    for r in range(2):
        outgoing[pl.ds(r * 16 + 15, DEVICES, stride=32), :] = jnp.zeros((DEVICES, 128), jnp.float32)

    @pl.loop(0, FIELDS)
    def _(f):
        for part in range(3):
            block = second[f, 4 * part:4 * part + 4].reshape(128, OWNED)
            high = block.astype(jnp.bfloat16)
            rest = block - high.astype(jnp.float32)
            middle = rest.astype(jnp.bfloat16)
            low = (rest - middle.astype(jnp.float32)).astype(jnp.bfloat16)
            moved = nt_dot(chosen, high) + nt_dot(chosen, middle) + nt_dot(chosen, low)
            for r in range(2):
                outgoing[pl.ds(f * 3 + part + r * 16, DEVICES, stride=32), :] = moved[
                    r * DEVICES:(r + 1) * DEVICES
                ]

    for f in range(FIELDS):
        rows = slice(f * LEVELS, (f + 1) * LEVELS)
        weighted[rows, :] = (weighted[rows, :] + profiles[rows, :]) * mass_rows
    weighted[60:72, :] = mass_rows
    weighted[72:128, :] = jnp.zeros((56, OWNED), jnp.float32)
    hrow = lax.broadcasted_iota(jnp.int32, (HALO_ROWS, OWNED), 0)
    hlane = lax.broadcasted_iota(jnp.int32, (HALO_ROWS, OWNED), 1)
    x_node = (hrow % 8 // 4) * 16 + hrow % 4
    y_node = ((hrow % 16) // 4) * 32 + (hrow % 4) * 4
    node = jnp.where(hrow < 8, x_node, x_node + 108)
    node = jnp.where(hrow < 16, node, jnp.where(hrow < 32, y_node, y_node + 19))
    corner = jnp.where(hrow == 48, 0, jnp.where(hrow == 56, 19, jnp.where(hrow == 64, 108, 127)))
    corner = jnp.where(hrow % 8 == 0, corner, -1)
    node = jnp.where(hrow < 48, node, corner)
    faces[...] = nt_dot(jnp.where(node == hlane, 1.0, 0.0), weighted[...], HIGHEST)

    pl.semaphore_wait(barrier, DEVICES - 1)
    face_copies = []
    for i, (at, rows, sx, sy) in enumerate(HALOS):
        copy = pltpu.make_async_remote_copy(
            src_ref=faces.at[pl.ds(at, rows)],
            dst_ref=halo.at[pl.ds(at, rows)],
            send_sem=face_send.at[i],
            recv_sem=face_recv.at[i],
            device_id=((ex + sx + N_EX) % N_EX, (ey + sy + N_EY) % N_EY),
            device_id_type=MESH,
        )
        copy.start()
        face_copies.append(copy)
    copies = []
    mine = pl.ds(pl.multiple_of(me * 32, 32), 32)
    for i, step in enumerate(STEPS):
        at_ex, at_ey = peer(step)
        there = pl.ds(pl.multiple_of((at_ex * N_EY + at_ey) * 32, 32), 32)
        copy = pltpu.make_async_remote_copy(
            src_ref=outgoing.at[there],
            dst_ref=landed.at[mine],
            send_sem=send_sem.at[i],
            recv_sem=recv_sem.at[i],
            device_id=(at_ex, at_ey),
            device_id_type=MESH,
        )
        copy.start()
        copies.append(copy)
    own = pltpu.make_async_copy(outgoing.at[mine], landed.at[mine], own_sem)
    own.start()

    def place(index):
        across = (index // 32) * 3 + index % 16 // 4
        along = (index // 16 % 2) * 3 + index % 4
        return across * 8 + along

    for copy in face_copies:
        copy.wait()
    shared = jnp.where(place(row) == place(lane), 1.0, 0.0)
    hside = jnp.where(hrow < 8, 96, 0) + (hrow % 8 // 4) * 3 + hrow % 4
    hfront = ((hrow % 16 // 4) * 3 + hrow % 4) * 8 + jnp.where(hrow < 32, 6, 0)
    hcorner = jnp.where(
        hrow == 48, 102, jnp.where(hrow == 56, 96, jnp.where(hrow == 64, 6, 0))
    )
    hcorner = jnp.where(hrow % 8 == 0, hcorner, -1)
    hplace = jnp.where(hrow < 16, hside, jnp.where(hrow < 48, hfront, hcorner))
    met = jnp.where(hplace == place(hlane), 1.0, 0.0)
    summed = jnp.dot(weighted[...], shared, precision=HIGHEST, preferred_element_type=jnp.float32)
    summed = summed + tn_dot(halo[...], met, HIGHEST)
    below = summed[60:72]
    for f in range(FIELDS):
        gcm_out[f] = jnp.swapaxes(summed[f * LEVELS:(f + 1) * LEVELS] / below, 0, 1)

    own.wait()
    for copy in copies:
        copy.wait()


def unpack_kernel(landed, gcm_in, cloud, gcm_out, held, laid, in_sem, out_sem):
    load = pltpu.make_async_copy(landed, held, in_sem)
    load.start()
    gcm_out[...] = gcm_in[...]
    load.wait()
    copies = []
    for f in range(FIELDS):
        for part in range(3):
            at = (f * 3 + part) * 128
            for r in range(2):
                block = held[pl.ds(f * 3 + part + r * 16, DEVICES, stride=32), :]
                laid[at:at + 128, r * 128:(r + 1) * 128] = block.T
        rows = pl.ds(f * 384, 384)
        copy = pltpu.make_async_copy(laid.at[rows], cloud.at[rows], out_sem.at[f])
        copy.start()
        copies.append(copy)
    for copy in copies:
        copy.wait()


def body(crm_state, gcm_state, mass, dest, cost_class):
    any_space = pl.BlockSpec(memory_space=pl.ANY)
    vmem = pl.BlockSpec(memory_space=pltpu.VMEM)
    gcm_rows = gcm_state.transpose(0, 2, 3, 4, 5, 1).reshape(FIELDS, OWNED, LEVELS)
    mass_rows = mass.transpose(1, 2, 3, 4, 0).reshape(OWNED, LEVELS)
    landed, gcm_out = pl.pallas_call(
        cloud_kernel,
        out_shape=(
            jax.ShapeDtypeStruct((DEVICES * 32, 128), jnp.float32),
            jax.ShapeDtypeStruct((FIELDS, OWNED, LEVELS), jnp.float32),
        ),
        in_specs=[any_space, vmem, vmem, vmem, vmem],
        out_specs=(any_space, vmem),
        scratch_shapes=[
            pltpu.VMEM((FIELDS, LEVELS + 2, WIDTH, OWNED), jnp.float32),
            pltpu.VMEM((FIELDS, LEVELS + 2, WIDTH, OWNED), jnp.float32),
            pltpu.VMEM((FIELDS, LEVELS, WIDTH, OWNED), jnp.float32),
            pltpu.VMEM((FIELDS * LEVELS, OWNED), jnp.float32),
            pltpu.VMEM((128, OWNED), jnp.float32),
            pltpu.VMEM((HALO_ROWS, 128), jnp.float32),
            pltpu.VMEM((HALO_ROWS, 128), jnp.float32),
            pltpu.VMEM((DEVICES * 32, 128), jnp.float32),
            pltpu.SemaphoreType.DMA,
            pltpu.SemaphoreType.DMA,
            pltpu.SemaphoreType.DMA((DEVICES - 1,)),
            pltpu.SemaphoreType.DMA((DEVICES - 1,)),
            pltpu.SemaphoreType.DMA((8,)),
            pltpu.SemaphoreType.DMA((8,)),
        ],
        compiler_params=pltpu.CompilerParams(
            collective_id=0, has_side_effects=True, vmem_limit_bytes=48 * 2**20
        ),
        name="clouds",
    )(crm_state, gcm_rows, mass_rows, dest.reshape(1, OWNED), cost_class.reshape(1, OWNED))
    cloud, gcm_out = pl.pallas_call(
        unpack_kernel,
        out_shape=(
            jax.ShapeDtypeStruct((FIELDS * LEVELS * WIDTH, 2 * DEVICES), jnp.float32),
            jax.ShapeDtypeStruct((FIELDS, OWNED, LEVELS), jnp.float32),
        ),
        in_specs=[any_space, vmem],
        out_specs=(any_space, vmem),
        scratch_shapes=[
            pltpu.VMEM((DEVICES * 32, 128), jnp.float32),
            pltpu.VMEM((FIELDS * LEVELS * WIDTH, 2 * DEVICES), jnp.float32),
            pltpu.SemaphoreType.DMA,
            pltpu.SemaphoreType.DMA((FIELDS,)),
        ],
        compiler_params=pltpu.CompilerParams(vmem_limit_bytes=48 * 2**20),
        name="unpack",
    )(landed, gcm_out)
    cloud = cloud.reshape(FIELDS, LEVELS, WIDTH, 2 * DEVICES)
    gcm_out = gcm_out.reshape(FIELDS, 4, 2, 4, 4, LEVELS).transpose(0, 5, 1, 2, 3, 4)
    return cloud, gcm_out


def solution(mesh):
    return jax.shard_map(
        body,
        mesh=mesh,
        in_specs=(
            P(None, None, None, ("ex", "ey")),
            P(None, None, "ex", "ey", None, None),
            P(None, "ex", "ey", None, None),
            P(("ex", "ey"), None),
            P(("ex", "ey")),
        ),
        out_specs=(P(None, None, None, ("ex", "ey")), P(None, None, "ex", "ey", None, None)),
        check_vma=False,
    )
```

profile of v0, /device:TPU:5, one launch (start us, length us, event | category | flops | bytes accessed | tf_op | source)
XLA Modules:
  0.0 47.0 jit_solution(9895225398597990601)
XLA Ops:
  0.6 0.0 copy-start
  0.6 1.2 %copy-done = f32[5,12,32,128]{3,2,1,0:T(8,128)S(1)} copy-done((f32[5,12,32,128]{3,2,1,0:T(8,128)S(1)}, f32[5,12,32,128]{3,2,1,0:T(8,128)}, u32[]{:S(2)}) %copy-start) | copy-done | bytes 983064
  1.8 0.0 copy-start.1
  1.8 1.0 %copy-done.1 = f32[5,12,4,2,4,4]{1,5,4,3,2,0:T(4,128)S(1)} copy-done((f32[5,12,4,2,4,4]{1,5,4,3,2,0:T(4,128)S(1)}, f32[5,12,4,2,4,4]{1,5,4,3,2,0:T(4,128)}, u32[]{:S(2)}) %copy-start.1) | copy-done | bytes 30744
  2.8 0.0 copy-start.2
  2.8 0.8 %copy-done.2 = f32[12,4,2,4,4]{0,4,3,2,1:T(4,128)S(1)} copy-done((f32[12,4,2,4,4]{0,4,3,2,1:T(4,128)S(1)}, f32[12,4,2,4,4]{0,4,3,2,1:T(4,128)}, u32[]{:S(2)}) %copy-start.2) | copy-done | bytes 6168
  3.6 0.0 copy-start.3
  3.6 0.7 %copy-done.3 = s32[128,1]{0,1:T(1,128)S(1)} copy-done((s32[128,1]{0,1:T(1,128)S(1)}, s32[128,1]{0,1:T(1,128)}, u32[]{:S(2)}) %copy-start.3) | copy-done | bytes 536
  4.3 0.0 copy-start.4
  4.3 0.7 %copy-done.4 = s32[128]{0:T(128)S(1)} copy-done((s32[128]{0:T(128)S(1)}, s32[128]{0:T(128)}, u32[]{:S(2)}) %copy-start.4) | copy-done | bytes 536
  5.0 39.2 %clouds.1 = (f32[4096,128]{1,0:T(8,128)S(1)}, f32[5,128,12]{2,1,0:T(8,128)S(1)}) custom-call(f32[5,12,32,128]{3,2,1,0:T(8,128)S(1)} %copy-done, f32[5,128,12]{2,1,0:T(8,128)S(1)} %bitcast.12, f32[128,12]{1,0:T(8,128)S(1)} %bitcast.13, s32[1,128]{1,0:T(1,128)S(1)} %bitcast.14, s32[1,128]{1,0:T(1,128)S(1)} %bitcast.15), custom_call_target="tpu_custom_call" | custom-call | tf_op jit(solution)/shard_map/clouds/pallas_call | solution.py:254
  44.2 2.8 %unpack.1 = (f32[1920,256]{1,0:T(8,128)}, f32[5,128,12]{2,1,0:T(8,128)}) custom-call(f32[4096,128]{1,0:T(8,128)S(1)} %get-tuple-element.6.landed, f32[5,128,12]{2,1,0:T(8,128)S(1)} %get-tuple-element.7.gcm_in), custom_call_target="tpu_custom_call" | custom-call | tf_op jit(solution)/shard_map/unpack/pallas_call | solution.py:283
Async XLA Ops:
  0.6 1.2 %copy-start = (f32[5,12,32,128]{3,2,1,0:T(8,128)S(1)}, f32[5,12,32,128]{3,2,1,0:T(8,128)}, u32[]{:S(2)}) copy-start(f32[5,12,32,128]{3,2,1,0:T(8,128)} %crm.1) | copy-start | bytes 2949124
  1.8 1.0 %copy-start.1 = (f32[5,12,4,2,4,4]{1,5,4,3,2,0:T(4,128)S(1)}, f32[5,12,4,2,4,4]{1,5,4,3,2,0:T(4,128)}, u32[]{:S(2)}) copy-start(f32[5,12,4,2,4,4]{1,5,4,3,2,0:T(4,128)} %param.6) | copy-start | bytes 92164
  2.8 0.8 %copy-start.2 = (f32[12,4,2,4,4]{0,4,3,2,1:T(4,128)S(1)}, f32[12,4,2,4,4]{0,4,3,2,1:T(4,128)}, u32[]{:S(2)}) copy-start(f32[12,4,2,4,4]{0,4,3,2,1:T(4,128)} %param.7) | copy-start | bytes 18436
  3.6 0.7 %copy-start.3 = (s32[128,1]{0,1:T(1,128)S(1)}, s32[128,1]{0,1:T(1,128)}, u32[]{:S(2)}) copy-start(s32[128,1]{0,1:T(1,128)} %param.8) | copy-start | bytes 1540
  4.3 0.7 %copy-start.4 = (s32[128]{0:T(128)S(1)}, s32[128]{0:T(128)}, u32[]{:S(2)}) copy-start(s32[128]{0:T(128)} %param.9) | copy-start | bytes 1540
where the time goes:
time: 47.3 us; the launch traced here: 47 us
  Pallas kernels  42 us (89%)
  local copies, waits for them, and re-layouts  4.32 us (9%)
  between operations  0.65 us (1%)
    pallas_call x1, Pallas kernels, body(): pl.pallas_call(cloud_kernel, out_shape=(jax.ShapeDtypeStruct((DEVICES * 3...  39.2 us
    unnamed x10, local copies, waits for them, and re-layouts  4.32 us
    pallas_call x1, Pallas kernels, body(): pl.pallas_call(unpack_kernel, out_shape=(jax.ShapeDtypeStruct((FIELDS * L...  2.84 us

commit v1 on v0

v1 whole, which is shorter than its diff:
```python
import functools
import random

import jax
import jax.numpy as jnp
from jax import lax
from jax.experimental import pallas as pl
from jax.experimental.pallas import tpu as pltpu
from jax.sharding import PartitionSpec as P

MESH = pl.DeviceIdType.MESH
HIGHEST = lax.Precision.HIGHEST
FIELDS, LEVELS, WIDTH, OWNED, DEVICES = 5, 12, 32, 128, 128
N_EX, N_EY = 16, 8
HALO_ROWS = 80
PIECE = 10
PART_ROWS = DEVICES * PIECE
HALOS = (
    (0, 8, -1, 0),
    (8, 8, 1, 0),
    (16, 16, 0, -1),
    (32, 16, 0, 1),
    (48, 8, -1, -1),
    (56, 8, -1, 1),
    (64, 8, 1, -1),
    (72, 8, 1, 1),
)


def far_first():
    steps = [
        (dx, dy, dz, dc)
        for dx in range(4)
        for dy in range(4)
        for dz in range(4)
        for dc in range(2)
    ][1:]
    random.Random(0).shuffle(steps)
    return sorted(steps, key=lambda s: -sum(min(v, 4 - v) for v in s[:3]))


STEPS = far_first()


def nt_dot(a, b, precision=None):
    return lax.dot_general(
        a, b, (((1,), (1,)), ((), ())), precision=precision, preferred_element_type=jnp.float32
    )


def tn_dot(a, b, precision=None):
    return lax.dot_general(
        a, b, (((0,), (0,)), ((), ())), precision=precision, preferred_element_type=jnp.float32
    )


def level_step(source, z, profiles, means):
    values = [source[f, z + 1, 8:40] for f in range(FIELDS)]
    drift = 0.075 * values[0]
    condensed = 0.4 * jnp.maximum(values[3], 0.0)
    after = []
    for f in range(FIELDS):
        s = values[f]
        west, east = source[f, z + 1, 7:39], source[f, z + 1, 9:41]
        mean = jnp.sum(s, axis=0, keepdims=True) * (1.0 / WIDTH)
        if means is not None:
            means[pl.ds(f * LEVELS + z, 1), :] = mean
        nudged = 0.5 * (profiles[pl.ds(f * LEVELS + z, 1), :] - mean)
        near = (east + west) + (source[f, z + 2, 8:40] + source[f, z, 8:40])
        kept = 0.4 if f == 4 else 0.6
        new = (kept * s + 0.1 * near) - drift * (east - west) + nudged
        if f == 1:
            new = new + 0.3 * values[2]
        elif f == 2:
            new = new - 0.3 * values[1] + 0.5 * condensed
        elif f == 3:
            new = new - condensed
        elif f == 4:
            new = new + condensed
        after.append(new)
    return values, after


def cloud_kernel(
    crm, gcm_hbm, mass_hbm, dest_hbm, cost_hbm, landed, gcm_out,
    start, first, second, profiles, means, weighted, faces, halo, outgoing,
    gcm, gcm_new, mass, dest, cost, load_sem, own_sem, send_sem, recv_sem, face_send, face_recv,
):
    ex, ey = lax.axis_index("ex"), lax.axis_index("ey")
    me = ex * N_EY + ey
    px, pz, py, pc = ex // 4, ex % 4, ey // 2, ey % 2

    at_ex = [[((px + dx) % 4) * 4 + (pz + dz) % 4 for dz in range(4)] for dx in range(4)]
    at_ey = [[((py + dy) % 4) * 2 + (pc + dc) % 2 for dc in range(2)] for dy in range(4)]

    def peer(step):
        dx, dy, dz, dc = step
        return at_ex[dx][dz], at_ey[dy][dc]

    loads = [
        pltpu.make_async_copy(source, into, load_sem.at[i])
        for i, (source, into) in enumerate(
            (
                (dest_hbm, dest),
                (gcm_hbm, gcm),
                (mass_hbm, mass),
                (cost_hbm, cost),
                (crm, start.at[:, pl.ds(1, LEVELS), pl.ds(8, WIDTH)]),
                (crm.at[:, :, pl.ds(WIDTH - 1, 1)], start.at[:, pl.ds(1, LEVELS), pl.ds(7, 1)]),
                (crm.at[:, :, pl.ds(0, 1)], start.at[:, pl.ds(1, LEVELS), pl.ds(40, 1)]),
            )
        )
    ]
    for load in loads:
        load.start()
    barrier = pltpu.get_barrier_semaphore()
    for step in STEPS:
        pl.semaphore_signal(barrier, inc=1, device_id=peer(step), device_id_type=MESH)

    loads[0].wait()
    row = lax.broadcasted_iota(jnp.int32, (OWNED, OWNED), 0)
    lane = lax.broadcasted_iota(jnp.int32, (OWNED, OWNED), 1)
    target = dest[...].astype(jnp.float32)
    target_rows = jnp.sum(jnp.where(row == lane, target, 0.0), axis=1, keepdims=True)
    earlier = jnp.where((target_rows == target) & (row < lane), 1.0, 0.0)
    slot = jnp.sum(earlier, axis=0, keepdims=True) * DEVICES + target
    slots = lax.broadcasted_iota(jnp.int32, (2 * DEVICES, OWNED), 0).astype(jnp.float32)
    chosen = jnp.where(slots == slot, 1.0, 0.0).astype(jnp.bfloat16)

    loads[1].wait()
    loads[2].wait()
    for f in range(FIELDS):
        profiles[f * LEVELS:(f + 1) * LEVELS, :] = jnp.swapaxes(gcm[f], 0, 1)
    mass_rows = jnp.swapaxes(mass[...], 0, 1)

    zero = jnp.zeros((WIDTH, OWNED), jnp.float32)
    for f in range(FIELDS):
        for z in (0, LEVELS + 1):
            start[f, z, 8:40] = zero
            first[f, z, 8:40] = zero
    for load in loads[3:]:
        load.wait()
    twice = cost[...].astype(jnp.float32) >= 2.0

    chosen_pair = jnp.concatenate([chosen, chosen], axis=1)

    def advance_once(first_level, last_level):
        @pl.loop(first_level, last_level)
        def _(z):
            _, after = level_step(start, z, profiles, means)
            for f in range(FIELDS):
                first[f, z + 1, 8:40] = after[f]
                first[f, z + 1, 7:8] = after[f][WIDTH - 1:]
                first[f, z + 1, 40:41] = after[f][:1]

    def advance_twice(first_level, last_level):
        @pl.loop(first_level, last_level, unroll=2)
        def _(z):
            values, after = level_step(first, z, profiles, None)
            for f in range(FIELDS):
                updated = jnp.where(twice, after[f], values[f])
                second[f, z] = updated
                at = pl.ds(f * LEVELS + z, 1)
                mean = jnp.sum(updated, axis=0, keepdims=True) * (1.0 / WIDTH)
                weighted[at, :] = mean - means[at, :]

    def select(part):
        for f in range(FIELDS):
            block = second[f, 4 * part:4 * part + 4].reshape(128, OWNED)
            high = block.astype(jnp.bfloat16)
            low = (block - high.astype(jnp.float32)).astype(jnp.bfloat16)
            moved = nt_dot(chosen_pair, jnp.concatenate([high, low], axis=1))
            for r in range(2):
                at = part * PART_ROWS + r * FIELDS + f
                outgoing[pl.ds(at, DEVICES, stride=PIECE), :] = moved[
                    r * DEVICES:(r + 1) * DEVICES
                ]

    def send(part):
        mine = pl.ds(part * PART_ROWS + me * PIECE, PIECE)
        for step in STEPS:
            there_ex, there_ey = peer(step)
            there = pl.ds(part * PART_ROWS + (there_ex * N_EY + there_ey) * PIECE, PIECE)
            pltpu.make_async_remote_copy(
                src_ref=outgoing.at[there],
                dst_ref=landed.at[mine],
                send_sem=send_sem,
                recv_sem=recv_sem,
                device_id=(there_ex, there_ey),
                device_id_type=MESH,
            ).start()
        own = pltpu.make_async_copy(outgoing.at[mine], landed.at[mine], own_sem.at[part])
        own.start()
        return own

    advance_once(0, 5)
    advance_twice(0, 4)
    select(0)
    pl.semaphore_wait(barrier, DEVICES - 1)
    owns = [send(0)]
    advance_once(5, 9)
    advance_twice(4, 8)
    select(1)
    owns.append(send(1))
    advance_once(9, 12)
    advance_twice(8, 12)
    select(2)

    for f in range(FIELDS):
        rows = slice(f * LEVELS, (f + 1) * LEVELS)
        weighted[rows, :] = (weighted[rows, :] + profiles[rows, :]) * mass_rows
    weighted[60:72, :] = mass_rows
    weighted[72:128, :] = jnp.zeros((56, OWNED), jnp.float32)
    hrow = lax.broadcasted_iota(jnp.int32, (HALO_ROWS, OWNED), 0)
    hlane = lax.broadcasted_iota(jnp.int32, (HALO_ROWS, OWNED), 1)
    x_node = (hrow % 8 // 4) * 16 + hrow % 4
    y_node = ((hrow % 16) // 4) * 32 + (hrow % 4) * 4
    node = jnp.where(hrow < 8, x_node, x_node + 108)
    node = jnp.where(hrow < 16, node, jnp.where(hrow < 32, y_node, y_node + 19))
    corner = jnp.where(hrow == 48, 0, jnp.where(hrow == 56, 19, jnp.where(hrow == 64, 108, 127)))
    corner = jnp.where(hrow % 8 == 0, corner, -1)
    node = jnp.where(hrow < 48, node, corner)
    faces[...] = nt_dot(jnp.where(node == hlane, 1.0, 0.0), weighted[...], HIGHEST)

    face_copies = []
    for i, (at, rows, sx, sy) in enumerate(HALOS):
        copy = pltpu.make_async_remote_copy(
            src_ref=faces.at[pl.ds(at, rows)],
            dst_ref=halo.at[pl.ds(at, rows)],
            send_sem=face_send.at[i],
            recv_sem=face_recv.at[i],
            device_id=((ex + sx + N_EX) % N_EX, (ey + sy + N_EY) % N_EY),
            device_id_type=MESH,
        )
        copy.start()
        face_copies.append(copy)
    owns.append(send(2))

    def place(index):
        across = (index // 32) * 3 + index % 16 // 4
        along = (index // 16 % 2) * 3 + index % 4
        return across * 8 + along

    for copy in face_copies:
        copy.wait()
    shared = jnp.where(place(row) == place(lane), 1.0, 0.0)
    hside = jnp.where(hrow < 8, 96, 0) + (hrow % 8 // 4) * 3 + hrow % 4
    hfront = ((hrow % 16 // 4) * 3 + hrow % 4) * 8 + jnp.where(hrow < 32, 6, 0)
    hcorner = jnp.where(
        hrow == 48, 102, jnp.where(hrow == 56, 96, jnp.where(hrow == 64, 6, 0))
    )
    hcorner = jnp.where(hrow % 8 == 0, hcorner, -1)
    hplace = jnp.where(hrow < 16, hside, jnp.where(hrow < 48, hfront, hcorner))
    met = jnp.where(hplace == place(hlane), 1.0, 0.0)
    summed = jnp.dot(weighted[...], shared, precision=HIGHEST, preferred_element_type=jnp.float32)
    summed = summed + tn_dot(halo[...], met, HIGHEST)
    below = summed[60:72]
    for f in range(FIELDS):
        gcm_new[f] = jnp.swapaxes(summed[f * LEVELS:(f + 1) * LEVELS] / below, 0, 1)

    store = pltpu.make_async_copy(gcm_new, gcm_out, load_sem.at[0])
    store.start()
    for own in owns:
        own.wait()
    store.wait()
    everything = pl.ds(0, 3 * (DEVICES - 1) * PIECE)
    pltpu.make_async_copy(outgoing.at[everything], outgoing.at[everything], send_sem).wait()
    pltpu.make_async_copy(landed.at[everything], landed.at[everything], recv_sem).wait()


def unpack_kernel(landed, gcm_in, cloud, gcm_out, held, gcm_held, laid, in_sem, out_sem):
    loads = []
    for part in range(3):
        rows = pl.ds(part * PART_ROWS, PART_ROWS)
        load = pltpu.make_async_copy(landed.at[rows], held.at[rows], in_sem.at[part])
        load.start()
        loads.append(load)
    gcm_load = pltpu.make_async_copy(gcm_in, gcm_held, in_sem.at[3])
    gcm_load.start()
    stores = []
    for part in range(3):
        loads[part].wait()
        for f in range(FIELDS):
            for r in range(2):
                at = part * PART_ROWS + r * FIELDS + f
                block = held[pl.ds(at, DEVICES, stride=PIECE), :]
                laid[f, part * 128:(part + 1) * 128, r * 128:(r + 1) * 128] = block.T
        rows = pl.ds(part * 128, 128)
        store = pltpu.make_async_copy(laid.at[:, rows], cloud.at[:, rows], out_sem.at[part])
        store.start()
        stores.append(store)
        if part == 0:
            gcm_load.wait()
            store = pltpu.make_async_copy(gcm_held, gcm_out, out_sem.at[3])
            store.start()
            stores.append(store)
    for store in stores:
        store.wait()


def body(crm_state, gcm_state, mass, dest, cost_class):
    any_space = pl.BlockSpec(memory_space=pl.ANY)
    gcm_rows = gcm_state.transpose(0, 2, 3, 4, 5, 1).reshape(FIELDS, OWNED, LEVELS)
    mass_rows = mass.transpose(1, 2, 3, 4, 0).reshape(OWNED, LEVELS)
    landed, gcm_out = pl.pallas_call(
        cloud_kernel,
        out_shape=(
            jax.ShapeDtypeStruct((3 * PART_ROWS, 128), jnp.float32),
            jax.ShapeDtypeStruct((FIELDS, OWNED, LEVELS), jnp.float32),
        ),
        in_specs=[pl.BlockSpec(memory_space=pltpu.HBM)] * 5,
        out_specs=(any_space, any_space),
        scratch_shapes=[
            pltpu.VMEM((FIELDS, LEVELS + 2, 48, OWNED), jnp.float32),
            pltpu.VMEM((FIELDS, LEVELS + 2, 48, OWNED), jnp.float32),
            pltpu.VMEM((FIELDS, LEVELS, WIDTH, OWNED), jnp.float32),
            pltpu.VMEM((FIELDS * LEVELS, OWNED), jnp.float32),
            pltpu.VMEM((FIELDS * LEVELS, OWNED), jnp.float32),
            pltpu.VMEM((128, OWNED), jnp.float32),
            pltpu.VMEM((HALO_ROWS, 128), jnp.float32),
            pltpu.VMEM((HALO_ROWS, 128), jnp.float32),
            pltpu.VMEM((3 * PART_ROWS, 128), jnp.float32),
            pltpu.VMEM((FIELDS, OWNED, LEVELS), jnp.float32),
            pltpu.VMEM((FIELDS, OWNED, LEVELS), jnp.float32),
            pltpu.VMEM((OWNED, LEVELS), jnp.float32),
            pltpu.VMEM((1, OWNED), jnp.int32),
            pltpu.VMEM((1, OWNED), jnp.int32),
            pltpu.SemaphoreType.DMA((7,)),
            pltpu.SemaphoreType.DMA((3,)),
            pltpu.SemaphoreType.DMA,
            pltpu.SemaphoreType.DMA,
            pltpu.SemaphoreType.DMA((8,)),
            pltpu.SemaphoreType.DMA((8,)),
        ],
        compiler_params=pltpu.CompilerParams(
            collective_id=0, has_side_effects=True, vmem_limit_bytes=67043328
        ),
        name="clouds",
    )(crm_state, gcm_rows, mass_rows, dest.reshape(1, OWNED), cost_class.reshape(1, OWNED))
    cloud, gcm_out = pl.pallas_call(
        unpack_kernel,
        out_shape=(
            jax.ShapeDtypeStruct((FIELDS, LEVELS * WIDTH, 2 * DEVICES), jnp.float32),
            jax.ShapeDtypeStruct((FIELDS, OWNED, LEVELS), jnp.float32),
        ),
        in_specs=[any_space, any_space],
        out_specs=(any_space, any_space),
        scratch_shapes=[
            pltpu.VMEM((3 * PART_ROWS, 128), jnp.float32),
            pltpu.VMEM((FIELDS, OWNED, LEVELS), jnp.float32),
            pltpu.VMEM((FIELDS, LEVELS * WIDTH, 2 * DEVICES), jnp.float32),
            pltpu.SemaphoreType.DMA((4,)),
            pltpu.SemaphoreType.DMA((4,)),
        ],
        compiler_params=pltpu.CompilerParams(vmem_limit_bytes=67043328),
        name="unpack",
    )(landed, gcm_out)
    cloud = cloud.reshape(FIELDS, LEVELS, WIDTH, 2 * DEVICES)
    gcm_out = gcm_out.reshape(FIELDS, 4, 2, 4, 4, LEVELS).transpose(0, 5, 1, 2, 3, 4)
    return cloud, gcm_out


def solution(mesh):
    return jax.shard_map(
        body,
        mesh=mesh,
        in_specs=(
            P(None, None, None, ("ex", "ey")),
            P(None, None, "ex", "ey", None, None),
            P(None, "ex", "ey", None, None),
            P(("ex", "ey"), None),
            P(("ex", "ey")),
        ),
        out_specs=(P(None, None, None, ("ex", "ey")), P(None, None, "ex", "ey", None, None)),
        check_vma=False,
    )
```

time: 47.3 us -> 39.3 us (0.83)
  the two profiles are of different devices: /device:TPU:5 before, /device:TPU:1 now
where the time goes in v1:
time: 39.3 us; the launch traced here: 39.2 us
  Pallas kernels  38.5 us (98%)
  between operations  0.64 us (2%)
    pallas_call x1, Pallas kernels, body(): pl.pallas_call(cloud_kernel, out_shape=(jax.ShapeDtypeStruct((3 * PART_RO...  35.6 us
    pallas_call x1, Pallas kernels, body(): pl.pallas_call(unpack_kernel, out_shape=(jax.ShapeDtypeStruct((FIELDS, LE...  2.94 us

profile of v1, /device:TPU:1, one launch (start us, length us, event | category | flops | bytes accessed | tf_op | source)
XLA Modules:
  0.0 39.2 jit_solution(15255640291039659216)
XLA Ops:
  0.6 35.6 %clouds.1 = (f32[3840,128]{1,0:T(8,128)}, f32[5,128,12]{2,1,0:T(8,128)}) custom-call(f32[5,12,32,128]{3,2,1,0:T(8,128)} %crm.1, f32[5,128,12]{2,1,0:T(8,128)} %bitcast.12, f32[128,12]{1,0:T(8,128)} %bitcast.13, s32[1,128]{1,0:T(1,128)} %bitcast.14, s32[1,128]{1,0:T(1,128)} %bitcast.15), custom_call_target="tpu_custom_call" | custom-call | tf_op jit(solution)/shard_map/clouds/pallas_call | solution.py:305
  36.2 2.9 %unpack.1 = (f32[5,384,256]{2,1,0:T(8,128)}, f32[5,128,12]{2,1,0:T(8,128)}) custom-call(f32[3840,128]{1,0:T(8,128)} %get-tuple-element.6.landed, f32[5,128,12]{2,1,0:T(8,128)} %get-tuple-element.7.gcm_in), custom_call_target="tpu_custom_call" | custom-call | tf_op jit(solution)/shard_map/unpack/pallas_call | solution.py:340

commit v2 on v1

--- a/solution.py
+++ b/solution.py
@@ -13,8 +13,8 @@
 FIELDS, LEVELS, WIDTH, OWNED, DEVICES = 5, 12, 32, 128, 128
 N_EX, N_EY = 16, 8
 HALO_ROWS = 80
-PIECE = 10
-PART_ROWS = DEVICES * PIECE
+BLOCKS = 6
+BLOCK_ROWS = DEVICES * FIELDS
 HALOS = (
     (0, 8, -1, 0),
     (8, 8, 1, 0),
@@ -40,6 +40,13 @@
 
 
 STEPS = far_first()
+X_STEPS = [(d, 0, 0, 0) for d in (2, 1, 3)]
+Y_STEPS = [(0, d, 0, 0) for d in (2, 1, 3)]
+Z_STEPS = [(0, 0, d, 0) for d in (2, 1, 3)]
+C_STEPS = [(0, 0, 0, 1)]
+NEAR_STEPS = [s for s in STEPS if sum(v != 0 for v in s[:3]) < 2]
+SIDE_STEPS = [s for s in STEPS if s not in NEAR_STEPS and 0 in s[1:3]]
+FAR_STEPS = [s for s in STEPS if 0 not in s[1:3]]
 
 
 def nt_dot(a, b, precision=None):
@@ -84,7 +91,7 @@
 def cloud_kernel(
     crm, gcm_hbm, mass_hbm, dest_hbm, cost_hbm, landed, gcm_out,
     start, first, second, profiles, means, weighted, faces, halo, outgoing,
-    gcm, gcm_new, mass, dest, cost, load_sem, own_sem, send_sem, recv_sem, face_send, face_recv,
+    gcm, gcm_new, mass, dest, cost, load_sem, stage_sem, own_sem, send_sem, recv_sem, face_send, face_recv,
 ):
     ex, ey = lax.axis_index("ex"), lax.axis_index("ey")
     me = ex * N_EY + ey
@@ -113,9 +120,12 @@
     ]
     for load in loads:
         load.start()
+    def signal(semaphore, steps):
+        for step in steps:
+            pl.semaphore_signal(semaphore, inc=1, device_id=peer(step), device_id_type=MESH)
+
     barrier = pltpu.get_barrier_semaphore()
-    for step in STEPS:
-        pl.semaphore_signal(barrier, inc=1, device_id=peer(step), device_id_type=MESH)
+    signal(barrier, X_STEPS + Y_STEPS + Z_STEPS + C_STEPS)
 
     loads[0].wait()
     row = lax.broadcasted_iota(jnp.int32, (OWNED, OWNED), 0)
@@ -171,37 +181,43 @@
             low = (block - high.astype(jnp.float32)).astype(jnp.bfloat16)
             moved = nt_dot(chosen_pair, jnp.concatenate([high, low], axis=1))
             for r in range(2):
-                at = part * PART_ROWS + r * FIELDS + f
-                outgoing[pl.ds(at, DEVICES, stride=PIECE), :] = moved[
+                outgoing[2 * part + r, pl.ds(f, DEVICES, stride=FIELDS), :] = moved[
                     r * DEVICES:(r + 1) * DEVICES
                 ]
 
-    def send(part):
-        mine = pl.ds(part * PART_ROWS + me * PIECE, PIECE)
-        for step in STEPS:
+    def piece(buffer, part, device):
+        return buffer.at[pl.ds(2 * part, 2), pl.ds(device * FIELDS, FIELDS)]
+
+    def send(part, steps):
+        for step in steps:
             there_ex, there_ey = peer(step)
-            there = pl.ds(part * PART_ROWS + (there_ex * N_EY + there_ey) * PIECE, PIECE)
             pltpu.make_async_remote_copy(
-                src_ref=outgoing.at[there],
-                dst_ref=landed.at[mine],
+                src_ref=piece(outgoing, part, there_ex * N_EY + there_ey),
+                dst_ref=piece(landed, part, me),
                 send_sem=send_sem,
                 recv_sem=recv_sem,
                 device_id=(there_ex, there_ey),
                 device_id_type=MESH,
             ).start()
-        own = pltpu.make_async_copy(outgoing.at[mine], landed.at[mine], own_sem.at[part])
-        own.start()
-        return own
-
+
+    pl.semaphore_wait(barrier, 10)
+    signal(stage_sem.at[0], C_STEPS)
     advance_once(0, 5)
+    pl.semaphore_wait(stage_sem.at[0], 1)
+    signal(stage_sem.at[1], X_STEPS)
     advance_twice(0, 4)
     select(0)
-    pl.semaphore_wait(barrier, DEVICES - 1)
-    owns = [send(0)]
+    send(0, NEAR_STEPS)
+    pl.semaphore_wait(stage_sem.at[1], 3)
+    signal(stage_sem.at[2], Y_STEPS)
+    send(0, SIDE_STEPS)
     advance_once(5, 9)
     advance_twice(4, 8)
     select(1)
-    owns.append(send(1))
+    send(1, NEAR_STEPS + SIDE_STEPS)
+    pl.semaphore_wait(stage_sem.at[2], 3)
+    send(0, FAR_STEPS)
+    send(1, FAR_STEPS)
     advance_once(9, 12)
     advance_twice(8, 12)
     select(2)
@@ -234,7 +250,14 @@
         )
         copy.start()
         face_copies.append(copy)
-    owns.append(send(2))
+    send(2, STEPS)
+    owns = []
+    for part in range(3):
+        own = pltpu.make_async_copy(
+            piece(outgoing, part, me), piece(landed, part, me), own_sem.at[part]
+        )
+        own.start()
+        owns.append(own)
 
     def place(index):
         across = (index // 32) * 3 + index % 16 // 4
@@ -263,37 +286,23 @@
     for own in owns:
         own.wait()
     store.wait()
-    everything = pl.ds(0, 3 * (DEVICES - 1) * PIECE)
-    pltpu.make_async_copy(outgoing.at[everything], outgoing.at[everything], send_sem).wait()
-    pltpu.make_async_copy(landed.at[everything], landed.at[everything], recv_sem).wait()
-
-
-def unpack_kernel(landed, gcm_in, cloud, gcm_out, held, gcm_held, laid, in_sem, out_sem):
-    loads = []
-    for part in range(3):
-        rows = pl.ds(part * PART_ROWS, PART_ROWS)
-        load = pltpu.make_async_copy(landed.at[rows], held.at[rows], in_sem.at[part])
-        load.start()
-        loads.append(load)
-    gcm_load = pltpu.make_async_copy(gcm_in, gcm_held, in_sem.at[3])
-    gcm_load.start()
-    stores = []
-    for part in range(3):
-        loads[part].wait()
+    others = pl.ds(0, (DEVICES - 1) * FIELDS)
+    pltpu.make_async_copy(outgoing.at[:, others], outgoing.at[:, others], send_sem).wait()
+    pltpu.make_async_copy(landed.at[:, others], landed.at[:, others], recv_sem).wait()
+
+
+def unpack_kernel(landed, gcm_in, cloud, gcm_out, laid, out_sem):
+    stores = [pltpu.make_async_copy(gcm_in, gcm_out, out_sem.at[BLOCKS])]
+    stores[0].start()
+    for block in range(BLOCKS):
+        rows, lanes = pl.ds(block // 2 * 128, 128), pl.ds(block % 2 * DEVICES, DEVICES)
         for f in range(FIELDS):
-            for r in range(2):
-                at = part * PART_ROWS + r * FIELDS + f
-                block = held[pl.ds(at, DEVICES, stride=PIECE), :]
-                laid[f, part * 128:(part + 1) * 128, r * 128:(r + 1) * 128] = block.T
-        rows = pl.ds(part * 128, 128)
-        store = pltpu.make_async_copy(laid.at[:, rows], cloud.at[:, rows], out_sem.at[part])
+            laid[f, rows, lanes] = landed[block, pl.ds(f, DEVICES, stride=FIELDS), :].T
+        store = pltpu.make_async_copy(
+            laid.at[:, rows, lanes], cloud.at[:, rows, lanes], out_sem.at[block]
+        )
         store.start()
         stores.append(store)
-        if part == 0:
-            gcm_load.wait()
-            store = pltpu.make_async_copy(gcm_held, gcm_out, out_sem.at[3])
-            store.start()
-            stores.append(store)
     for store in stores:
         store.wait()
 
@@ -305,7 +314,7 @@
     landed, gcm_out = pl.pallas_call(
         cloud_kernel,
         out_shape=(
-            jax.ShapeDtypeStruct((3 * PART_ROWS, 128), jnp.float32),
+            jax.ShapeDtypeStruct((BLOCKS, BLOCK_ROWS, 128), jnp.float32),
             jax.ShapeDtypeStruct((FIELDS, OWNED, LEVELS), jnp.float32),
         ),
         in_specs=[pl.BlockSpec(memory_space=pltpu.HBM)] * 5,
@@ -319,13 +328,14 @@
             pltpu.VMEM((128, OWNED), jnp.float32),
             pltpu.VMEM((HALO_ROWS, 128), jnp.float32),
             pltpu.VMEM((HALO_ROWS, 128), jnp.float32),
-            pltpu.VMEM((3 * PART_ROWS, 128), jnp.float32),
+            pltpu.VMEM((BLOCKS, BLOCK_ROWS, 128), jnp.float32),
             pltpu.VMEM((FIELDS, OWNED, LEVELS), jnp.float32),
             pltpu.VMEM((FIELDS, OWNED, LEVELS), jnp.float32),
             pltpu.VMEM((OWNED, LEVELS), jnp.float32),
             pltpu.VMEM((1, OWNED), jnp.int32),
             pltpu.VMEM((1, OWNED), jnp.int32),
             pltpu.SemaphoreType.DMA((7,)),
+            pltpu.SemaphoreType.REGULAR((3,)),
             pltpu.SemaphoreType.DMA((3,)),
             pltpu.SemaphoreType.DMA,
             pltpu.SemaphoreType.DMA,
@@ -333,26 +343,23 @@
             pltpu.SemaphoreType.DMA((8,)),
         ],
         compiler_params=pltpu.CompilerParams(
-            collective_id=0, has_side_effects=True, vmem_limit_bytes=67043328
+            collective_id=0, has_side_effects=True, vmem_limit_bytes=40 * 2**20
         ),
         name="clouds",
-    )(crm_state, gcm_rows, mass_rows, dest.reshape(1, OWNED), cost_class.reshape(1, OWNED))
+    )(*(pltpu.with_memory_space_constraint(v, pltpu.HBM) for v in (crm_state, gcm_rows, mass_rows, dest.reshape(1, OWNED), cost_class.reshape(1, OWNED))))
     cloud, gcm_out = pl.pallas_call(
         unpack_kernel,
         out_shape=(
             jax.ShapeDtypeStruct((FIELDS, LEVELS * WIDTH, 2 * DEVICES), jnp.float32),
             jax.ShapeDtypeStruct((FIELDS, OWNED, LEVELS), jnp.float32),
         ),
-        in_specs=[any_space, any_space],
+        in_specs=[pl.BlockSpec(memory_space=pltpu.VMEM), pl.BlockSpec(memory_space=pltpu.VMEM)],
         out_specs=(any_space, any_space),
         scratch_shapes=[
-            pltpu.VMEM((3 * PART_ROWS, 128), jnp.float32),
-            pltpu.VMEM((FIELDS, OWNED, LEVELS), jnp.float32),
             pltpu.VMEM((FIELDS, LEVELS * WIDTH, 2 * DEVICES), jnp.float32),
-            pltpu.SemaphoreType.DMA((4,)),
-            pltpu.SemaphoreType.DMA((4,)),
+            pltpu.SemaphoreType.DMA((BLOCKS + 1,)),
         ],
-        compiler_params=pltpu.CompilerParams(vmem_limit_bytes=67043328),
+        compiler_params=pltpu.CompilerParams(vmem_limit_bytes=16 * 2**20),
         name="unpack",
     )(landed, gcm_out)
     cloud = cloud.reshape(FIELDS, LEVELS, WIDTH, 2 * DEVICES)

time: 39.3 us -> 37.7 us (0.959)
  Pallas kernels: 38.5 us -> 36.9 us
    pallas_call x1, Pallas kernels: 2.94 us -> 1.8 us  [body(): pl.pallas_call(unpack_kernel, out_shape=(jax.ShapeDtypeStruct((FIELDS, LE...]
    pallas_call x1, Pallas kernels: 35.6 us -> 35.1 us  [body(): pl.pallas_call(cloud_kernel, out_shape=(jax.ShapeDtypeStruct((BLOCKS, BLO...]
where the time goes in v2:
time: 37.7 us; the launch traced here: 37.6 us
  Pallas kernels  36.9 us (98%)
  between operations  0.64 us (2%)
    pallas_call x1, Pallas kernels, body(): pl.pallas_call(cloud_kernel, out_shape=(jax.ShapeDtypeStruct((BLOCKS, BLO...  35.1 us
    pallas_call x1, Pallas kernels, body(): pl.pallas_call(unpack_kernel, out_shape=(jax.ShapeDtypeStruct((FIELDS, LE...  1.8 us

profile of v2, /device:TPU:1, one launch (start us, length us, event | category | flops | bytes accessed | tf_op | source)
XLA Modules:
  0.0 37.6 jit_solution(6393322501945030581)
XLA Ops:
  0.6 35.1 %clouds.1 = (f32[6,640,128]{2,1,0:T(8,128)S(1)}, f32[5,128,12]{2,1,0:T(8,128)S(1)}) custom-call(f32[5,12,32,128]{3,2,1,0:T(8,128)} %crm.1, f32[5,128,12]{2,1,0:T(8,128)} %bitcast.12, f32[128,12]{1,0:T(8,128)} %bitcast.13, s32[1,128]{1,0:T(1,128)} %bitcast.14, s32[1,128]{1,0:T(1,128)} %bitcast.15), custom_call_target="tpu_custom_call" | custom-call | tf_op jit(solution)/shard_map/clouds/pallas_call | solution.py:314
  35.8 1.8 %unpack.1 = (f32[5,384,256]{2,1,0:T(8,128)}, f32[5,128,12]{2,1,0:T(8,128)}) custom-call(f32[6,640,128]{2,1,0:T(8,128)S(1)} %get-tuple-element.6.landed, f32[5,128,12]{2,1,0:T(8,128)S(1)} %get-tuple-element.7.gcm_in), custom_call_target="tpu_custom_call" | custom-call | tf_op jit(solution)/shard_map/unpack/pallas_call | solution.py:350

commit v3 on v2

--- a/solution.py
+++ b/solution.py
@@ -45,8 +45,8 @@
 Z_STEPS = [(0, 0, d, 0) for d in (2, 1, 3)]
 C_STEPS = [(0, 0, 0, 1)]
 NEAR_STEPS = [s for s in STEPS if sum(v != 0 for v in s[:3]) < 2]
-SIDE_STEPS = [s for s in STEPS if s not in NEAR_STEPS and 0 in s[1:3]]
-FAR_STEPS = [s for s in STEPS if 0 not in s[1:3]]
+SIDE_STEPS = [s for s in STEPS if s not in NEAR_STEPS and 0 in s[:3]]
+FAR_STEPS = [s for s in STEPS if 0 not in s[:3]]
 
 
 def nt_dot(a, b, precision=None):
@@ -204,11 +204,11 @@
     signal(stage_sem.at[0], C_STEPS)
     advance_once(0, 5)
     pl.semaphore_wait(stage_sem.at[0], 1)
-    signal(stage_sem.at[1], X_STEPS)
+    signal(stage_sem.at[1], X_STEPS + Y_STEPS + Z_STEPS)
     advance_twice(0, 4)
     select(0)
     send(0, NEAR_STEPS)
-    pl.semaphore_wait(stage_sem.at[1], 3)
+    pl.semaphore_wait(stage_sem.at[1], 9)
     signal(stage_sem.at[2], Y_STEPS)
     send(0, SIDE_STEPS)
     advance_once(5, 9)
@@ -292,17 +292,19 @@
 
 
 def unpack_kernel(landed, gcm_in, cloud, gcm_out, laid, out_sem):
-    stores = [pltpu.make_async_copy(gcm_in, gcm_out, out_sem.at[BLOCKS])]
+    stores = [pltpu.make_async_copy(gcm_in, gcm_out, out_sem.at[15])]
     stores[0].start()
-    for block in range(BLOCKS):
-        rows, lanes = pl.ds(block // 2 * 128, 128), pl.ds(block % 2 * DEVICES, DEVICES)
+    for part in range(3):
         for f in range(FIELDS):
-            laid[f, rows, lanes] = landed[block, pl.ds(f, DEVICES, stride=FIELDS), :].T
-        store = pltpu.make_async_copy(
-            laid.at[:, rows, lanes], cloud.at[:, rows, lanes], out_sem.at[block]
-        )
-        store.start()
-        stores.append(store)
+            rows = pl.ds(part * 128, 128)
+            for r in range(2):
+                lanes = pl.ds(r * DEVICES, DEVICES)
+                laid[f, rows, lanes] = landed[2 * part + r, pl.ds(f, DEVICES, stride=FIELDS), :].T
+            store = pltpu.make_async_copy(
+                laid.at[f, rows], cloud.at[f, rows], out_sem.at[part * FIELDS + f]
+            )
+            store.start()
+            stores.append(store)
     for store in stores:
         store.wait()
 
@@ -357,7 +359,7 @@
         out_specs=(any_space, any_space),
         scratch_shapes=[
             pltpu.VMEM((FIELDS, LEVELS * WIDTH, 2 * DEVICES), jnp.float32),
-            pltpu.SemaphoreType.DMA((BLOCKS + 1,)),
+            pltpu.SemaphoreType.DMA((16,)),
         ],
         compiler_params=pltpu.CompilerParams(vmem_limit_bytes=16 * 2**20),
         name="unpack",

time: 37.7 us -> 36.3 us (0.963)
  Pallas kernels: 36.9 us -> 35.5 us
    pallas_call x1, Pallas kernels: 35.1 us -> 34 us  [body(): pl.pallas_call(cloud_kernel, out_shape=(jax.ShapeDtypeStruct((BLOCKS, BLO...]
where the time goes in v3:
time: 36.3 us; the launch traced here: 36.2 us
  Pallas kernels  35.5 us (98%)
  between operations  0.64 us (2%)
    pallas_call x1, Pallas kernels, body(): pl.pallas_call(cloud_kernel, out_shape=(jax.ShapeDtypeStruct((BLOCKS, BLO...  34 us
    pallas_call x1, Pallas kernels, body(): pl.pallas_call(unpack_kernel, out_shape=(jax.ShapeDtypeStruct((FIELDS, LE...  1.51 us

profile of v3, /device:TPU:1, one launch (start us, length us, event | category | flops | bytes accessed | tf_op | source)
XLA Modules:
  0.0 36.2 jit_solution(7588179143337132761)
XLA Ops:
  0.6 34.0 %clouds.1 = (f32[6,640,128]{2,1,0:T(8,128)S(1)}, f32[5,128,12]{2,1,0:T(8,128)S(1)}) custom-call(f32[5,12,32,128]{3,2,1,0:T(8,128)} %crm.1, f32[5,128,12]{2,1,0:T(8,128)} %bitcast.12, f32[128,12]{1,0:T(8,128)} %bitcast.13, s32[1,128]{1,0:T(1,128)} %bitcast.14, s32[1,128]{1,0:T(1,128)} %bitcast.15), custom_call_target="tpu_custom_call" | custom-call | tf_op jit(solution)/shard_map/clouds/pallas_call | solution.py:316
  34.7 1.5 %unpack.1 = (f32[5,384,256]{2,1,0:T(8,128)}, f32[5,128,12]{2,1,0:T(8,128)}) custom-call(f32[6,640,128]{2,1,0:T(8,128)S(1)} %get-tuple-element.6.landed, f32[5,128,12]{2,1,0:T(8,128)S(1)} %get-tuple-element.7.gcm_in), custom_call_target="tpu_custom_call" | custom-call | tf_op jit(solution)/shard_map/unpack/pallas_call | solution.py:352

commit v4 on v3

--- a/solution.py
+++ b/solution.py
@@ -43,10 +43,12 @@
 X_STEPS = [(d, 0, 0, 0) for d in (2, 1, 3)]
 Y_STEPS = [(0, d, 0, 0) for d in (2, 1, 3)]
 Z_STEPS = [(0, 0, d, 0) for d in (2, 1, 3)]
-C_STEPS = [(0, 0, 0, 1)]
 NEAR_STEPS = [s for s in STEPS if sum(v != 0 for v in s[:3]) < 2]
 SIDE_STEPS = [s for s in STEPS if s not in NEAR_STEPS and 0 in s[:3]]
 FAR_STEPS = [s for s in STEPS if 0 not in s[:3]]
+
+CHIPS = [s[:3] for s in STEPS if s[3] == 0]
+CORE_STEPS = [(*chip, None, core) for core in (1, 0) for chip in CHIPS] + [(0, 0, 0, 1)]
 
 
 def nt_dot(a, b, precision=None):
@@ -101,7 +103,9 @@
     at_ey = [[((py + dy) % 4) * 2 + (pc + dc) % 2 for dc in range(2)] for dy in range(4)]
 
     def peer(step):
-        dx, dy, dz, dc = step
+        dx, dy, dz, dc, *core = step
+        if core:
+            return at_ex[dx][dz], (py + dy) % 4 * 2 + core[0]
         return at_ex[dx][dz], at_ey[dy][dc]
 
     loads = [
@@ -112,9 +116,10 @@
                 (gcm_hbm, gcm),
                 (mass_hbm, mass),
                 (cost_hbm, cost),
-                (crm, start.at[:, pl.ds(1, LEVELS), pl.ds(8, WIDTH)]),
+                (crm.at[:, pl.ds(0, 6)], start.at[:, pl.ds(1, 6), pl.ds(8, WIDTH)]),
                 (crm.at[:, :, pl.ds(WIDTH - 1, 1)], start.at[:, pl.ds(1, LEVELS), pl.ds(7, 1)]),
                 (crm.at[:, :, pl.ds(0, 1)], start.at[:, pl.ds(1, LEVELS), pl.ds(40, 1)]),
+                (crm.at[:, pl.ds(6, 6)], start.at[:, pl.ds(7, 6), pl.ds(8, WIDTH)]),
             )
         )
     ]
@@ -125,7 +130,7 @@
             pl.semaphore_signal(semaphore, inc=1, device_id=peer(step), device_id_type=MESH)
 
     barrier = pltpu.get_barrier_semaphore()
-    signal(barrier, X_STEPS + Y_STEPS + Z_STEPS + C_STEPS)
+    signal(barrier, NEAR_STEPS)
 
     loads[0].wait()
     row = lax.broadcasted_iota(jnp.int32, (OWNED, OWNED), 0)
@@ -148,7 +153,7 @@
         for z in (0, LEVELS + 1):
             start[f, z, 8:40] = zero
             first[f, z, 8:40] = zero
-    for load in loads[3:]:
+    for load in loads[3:7]:
         load.wait()
     twice = cost[...].astype(jnp.float32) >= 2.0
 
@@ -185,8 +190,9 @@
                     r * DEVICES:(r + 1) * DEVICES
                 ]
 
-    def piece(buffer, part, device):
-        return buffer.at[pl.ds(2 * part, 2), pl.ds(device * FIELDS, FIELDS)]
+    def piece(buffer, group, device):
+        blocks = pl.ds(2, 4) if group else pl.ds(0, 2)
+        return buffer.at[blocks, pl.ds(device * FIELDS, FIELDS)]
 
     def send(part, steps):
         for step in steps:
@@ -200,28 +206,22 @@
                 device_id_type=MESH,
             ).start()
 
-    pl.semaphore_wait(barrier, 10)
-    signal(stage_sem.at[0], C_STEPS)
+    pl.semaphore_wait(barrier, len(NEAR_STEPS))
+    signal(stage_sem.at[0], X_STEPS + Y_STEPS + Z_STEPS)
     advance_once(0, 5)
-    pl.semaphore_wait(stage_sem.at[0], 1)
-    signal(stage_sem.at[1], X_STEPS + Y_STEPS + Z_STEPS)
     advance_twice(0, 4)
     select(0)
     send(0, NEAR_STEPS)
-    pl.semaphore_wait(stage_sem.at[1], 9)
-    signal(stage_sem.at[2], Y_STEPS)
+    pl.semaphore_wait(stage_sem.at[0], 9)
+    signal(stage_sem.at[1], Y_STEPS)
     send(0, SIDE_STEPS)
-    advance_once(5, 9)
-    advance_twice(4, 8)
+    loads[7].wait()
+    advance_once(5, 12)
+    advance_twice(4, 12)
     select(1)
-    send(1, NEAR_STEPS + SIDE_STEPS)
-    pl.semaphore_wait(stage_sem.at[2], 3)
+    select(2)
+    pl.semaphore_wait(stage_sem.at[1], 3)
     send(0, FAR_STEPS)
-    send(1, FAR_STEPS)
-    advance_once(9, 12)
-    advance_twice(8, 12)
-    select(2)
-
     for f in range(FIELDS):
         rows = slice(f * LEVELS, (f + 1) * LEVELS)
         weighted[rows, :] = (weighted[rows, :] + profiles[rows, :]) * mass_rows
@@ -250,9 +250,9 @@
         )
         copy.start()
         face_copies.append(copy)
-    send(2, STEPS)
+    send(1, CORE_STEPS)
     owns = []
-    for part in range(3):
+    for part in range(2):
         own = pltpu.make_async_copy(
             piece(outgoing, part, me), piece(landed, part, me), own_sem.at[part]
         )
@@ -336,8 +336,8 @@
             pltpu.VMEM((OWNED, LEVELS), jnp.float32),
             pltpu.VMEM((1, OWNED), jnp.int32),
             pltpu.VMEM((1, OWNED), jnp.int32),
-            pltpu.SemaphoreType.DMA((7,)),
-            pltpu.SemaphoreType.REGULAR((3,)),
+            pltpu.SemaphoreType.DMA((8,)),
+            pltpu.SemaphoreType.REGULAR((2,)),
             pltpu.SemaphoreType.DMA((3,)),
             pltpu.SemaphoreType.DMA,
             pltpu.SemaphoreType.DMA,

time: 36.3 us -> 35.5 us (0.978)
  Pallas kernels: 35.5 us -> 34.7 us
    pallas_call x1, Pallas kernels: 34 us -> 33.2 us  [body(): pl.pallas_call(cloud_kernel, out_shape=(jax.ShapeDtypeStruct((BLOCKS, BLO...]
where the time goes in v4:
time: 35.5 us; the launch traced here: 35.4 us
  Pallas kernels  34.7 us (98%)
  between operations  0.64 us (2%)
    pallas_call x1, Pallas kernels, body(): pl.pallas_call(cloud_kernel, out_shape=(jax.ShapeDtypeStruct((BLOCKS, BLO...  33.2 us
    pallas_call x1, Pallas kernels, body(): pl.pallas_call(unpack_kernel, out_shape=(jax.ShapeDtypeStruct((FIELDS, LE...  1.51 us

profile of v4, /device:TPU:1, one launch (start us, length us, event | category | flops | bytes accessed | tf_op | source)
XLA Modules:
  0.0 35.4 jit_solution(14427877587479297564)
XLA Ops:
  0.6 33.2 %clouds.1 = (f32[6,640,128]{2,1,0:T(8,128)S(1)}, f32[5,128,12]{2,1,0:T(8,128)S(1)}) custom-call(f32[5,12,32,128]{3,2,1,0:T(8,128)} %crm.1, f32[5,128,12]{2,1,0:T(8,128)} %bitcast.12, f32[128,12]{1,0:T(8,128)} %bitcast.13, s32[1,128]{1,0:T(1,128)} %bitcast.14, s32[1,128]{1,0:T(1,128)} %bitcast.15), custom_call_target="tpu_custom_call" | custom-call | tf_op jit(solution)/shard_map/clouds/pallas_call | solution.py:316
  33.9 1.5 %unpack.1 = (f32[5,384,256]{2,1,0:T(8,128)}, f32[5,128,12]{2,1,0:T(8,128)}) custom-call(f32[6,640,128]{2,1,0:T(8,128)S(1)} %get-tuple-element.6.landed, f32[5,128,12]{2,1,0:T(8,128)S(1)} %get-tuple-element.7.gcm_in), custom_call_target="tpu_custom_call" | custom-call | tf_op jit(solution)/shard_map/unpack/pallas_call | solution.py:352

commit v5 on v4

--- a/solution.py
+++ b/solution.py
@@ -48,7 +48,12 @@
 FAR_STEPS = [s for s in STEPS if 0 not in s[:3]]
 
 CHIPS = [s[:3] for s in STEPS if s[3] == 0]
-CORE_STEPS = [(*chip, None, core) for core in (1, 0) for chip in CHIPS] + [(0, 0, 0, 1)]
+CORE_STEPS = [
+    (*chip, None, core)
+    for chips in (CHIPS[:32], CHIPS[32:])
+    for core in (1, 0)
+    for chip in chips
+] + [(0, 0, 0, 1)]
 
 
 def nt_dot(a, b, precision=None):
@@ -238,34 +243,28 @@
     node = jnp.where(hrow < 48, node, corner)
     faces[...] = nt_dot(jnp.where(node == hlane, 1.0, 0.0), weighted[...], HIGHEST)
 
-    face_copies = []
     for i, (at, rows, sx, sy) in enumerate(HALOS):
         copy = pltpu.make_async_remote_copy(
             src_ref=faces.at[pl.ds(at, rows)],
             dst_ref=halo.at[pl.ds(at, rows)],
-            send_sem=face_send.at[i],
-            recv_sem=face_recv.at[i],
+            send_sem=face_send,
+            recv_sem=face_recv,
             device_id=((ex + sx + N_EX) % N_EX, (ey + sy + N_EY) % N_EY),
             device_id_type=MESH,
         )
         copy.start()
-        face_copies.append(copy)
     send(1, CORE_STEPS)
-    owns = []
-    for part in range(2):
-        own = pltpu.make_async_copy(
-            piece(outgoing, part, me), piece(landed, part, me), own_sem.at[part]
-        )
-        own.start()
-        owns.append(own)
+    mine = pl.ds(me * FIELDS, FIELDS)
+    own = pltpu.make_async_copy(outgoing.at[:, mine], landed.at[:, mine], own_sem)
+    own.start()
 
     def place(index):
         across = (index // 32) * 3 + index % 16 // 4
         along = (index // 16 % 2) * 3 + index % 4
         return across * 8 + along
 
-    for copy in face_copies:
-        copy.wait()
+    pltpu.make_async_copy(faces, faces, face_send).wait()
+    pltpu.make_async_copy(halo, halo, face_recv).wait()
     shared = jnp.where(place(row) == place(lane), 1.0, 0.0)
     hside = jnp.where(hrow < 8, 96, 0) + (hrow % 8 // 4) * 3 + hrow % 4
     hfront = ((hrow % 16 // 4) * 3 + hrow % 4) * 8 + jnp.where(hrow < 32, 6, 0)
@@ -283,30 +282,25 @@
 
     store = pltpu.make_async_copy(gcm_new, gcm_out, load_sem.at[0])
     store.start()
-    for own in owns:
-        own.wait()
+    own.wait()
     store.wait()
     others = pl.ds(0, (DEVICES - 1) * FIELDS)
     pltpu.make_async_copy(outgoing.at[:, others], outgoing.at[:, others], send_sem).wait()
     pltpu.make_async_copy(landed.at[:, others], landed.at[:, others], recv_sem).wait()
 
 
-def unpack_kernel(landed, gcm_in, cloud, gcm_out, laid, out_sem):
-    stores = [pltpu.make_async_copy(gcm_in, gcm_out, out_sem.at[15])]
-    stores[0].start()
+def unpack_kernel(landed, gcm_in, cloud, gcm_out, laid, gcm_sem, out_sem):
+    gcm_store = pltpu.make_async_copy(gcm_in, gcm_out, gcm_sem)
+    gcm_store.start()
     for part in range(3):
         for f in range(FIELDS):
             rows = pl.ds(part * 128, 128)
             for r in range(2):
                 lanes = pl.ds(r * DEVICES, DEVICES)
                 laid[f, rows, lanes] = landed[2 * part + r, pl.ds(f, DEVICES, stride=FIELDS), :].T
-            store = pltpu.make_async_copy(
-                laid.at[f, rows], cloud.at[f, rows], out_sem.at[part * FIELDS + f]
-            )
-            store.start()
-            stores.append(store)
-    for store in stores:
-        store.wait()
+            pltpu.make_async_copy(laid.at[f, rows], cloud.at[f, rows], out_sem).start()
+    gcm_store.wait()
+    pltpu.make_async_copy(laid, cloud, out_sem).wait()
 
 
 def body(crm_state, gcm_state, mass, dest, cost_class):
@@ -338,11 +332,11 @@
             pltpu.VMEM((1, OWNED), jnp.int32),
             pltpu.SemaphoreType.DMA((8,)),
             pltpu.SemaphoreType.REGULAR((2,)),
-            pltpu.SemaphoreType.DMA((3,)),
-            pltpu.SemaphoreType.DMA,
-            pltpu.SemaphoreType.DMA,
-            pltpu.SemaphoreType.DMA((8,)),
-            pltpu.SemaphoreType.DMA((8,)),
+            pltpu.SemaphoreType.DMA,
+            pltpu.SemaphoreType.DMA,
+            pltpu.SemaphoreType.DMA,
+            pltpu.SemaphoreType.DMA,
+            pltpu.SemaphoreType.DMA,
         ],
         compiler_params=pltpu.CompilerParams(
             collective_id=0, has_side_effects=True, vmem_limit_bytes=40 * 2**20
@@ -359,7 +353,8 @@
         out_specs=(any_space, any_space),
         scratch_shapes=[
             pltpu.VMEM((FIELDS, LEVELS * WIDTH, 2 * DEVICES), jnp.float32),
-            pltpu.SemaphoreType.DMA((16,)),
+            pltpu.SemaphoreType.DMA,
+            pltpu.SemaphoreType.DMA,
         ],
         compiler_params=pltpu.CompilerParams(vmem_limit_bytes=16 * 2**20),
         name="unpack",

time: 35.5 us -> 35.3 us (level)
  no operation moved by 1% of the time
where the time goes in v5:
time: 35.3 us; the launch traced here: 35.2 us
  Pallas kernels  34.5 us (98%)
  between operations  0.64 us (2%)
    pallas_call x1, Pallas kernels, body(): pl.pallas_call(cloud_kernel, out_shape=(jax.ShapeDtypeStruct((BLOCKS, BLO...  33 us
    pallas_call x1, Pallas kernels, body(): pl.pallas_call(unpack_kernel, out_shape=(jax.ShapeDtypeStruct((FIELDS, LE...  1.48 us

profile of v5, /device:TPU:1, one launch (start us, length us, event | category | flops | bytes accessed | tf_op | source)
XLA Modules:
  0.0 35.2 jit_solution(11585225455402912804)
XLA Ops:
  0.6 33.0 %clouds.1 = (f32[6,640,128]{2,1,0:T(8,128)S(1)}, f32[5,128,12]{2,1,0:T(8,128)S(1)}) custom-call(f32[5,12,32,128]{3,2,1,0:T(8,128)} %crm.1, f32[5,128,12]{2,1,0:T(8,128)} %bitcast.12, f32[128,12]{1,0:T(8,128)} %bitcast.13, s32[1,128]{1,0:T(1,128)} %bitcast.14, s32[1,128]{1,0:T(1,128)} %bitcast.15), custom_call_target="tpu_custom_call" | custom-call | tf_op jit(solution)/shard_map/clouds/pallas_call | solution.py:310
  33.7 1.5 %unpack.1 = (f32[5,384,256]{2,1,0:T(8,128)}, f32[5,128,12]{2,1,0:T(8,128)}) custom-call(f32[6,640,128]{2,1,0:T(8,128)S(1)} %get-tuple-element.6.landed, f32[5,128,12]{2,1,0:T(8,128)S(1)} %get-tuple-element.7.gcm_in), custom_call_target="tpu_custom_call" | custom-call | tf_op jit(solution)/shard_map/unpack/pallas_call | solution.py:346

commit v6 on v5

--- a/solution.py
+++ b/solution.py
@@ -14,16 +14,17 @@
 N_EX, N_EY = 16, 8
 HALO_ROWS = 80
 BLOCKS = 6
+SEMAPHORE_OF = (0, 1, 2, 3, 4, 4, 4, 5)
 BLOCK_ROWS = DEVICES * FIELDS
 HALOS = (
     (0, 8, -1, 0),
     (8, 8, 1, 0),
     (16, 16, 0, -1),
     (32, 16, 0, 1),
-    (48, 8, -1, -1),
-    (56, 8, -1, 1),
-    (64, 8, 1, -1),
-    (72, 8, 1, 1),
+    (48, 1, -1, -1),
+    (56, 1, -1, 1),
+    (64, 1, 1, -1),
+    (72, 1, 1, 1),
 )
 
 
@@ -114,7 +115,7 @@
         return at_ex[dx][dz], at_ey[dy][dc]
 
     loads = [
-        pltpu.make_async_copy(source, into, load_sem.at[i])
+        pltpu.make_async_copy(source, into, load_sem.at[SEMAPHORE_OF[i]])
         for i, (source, into) in enumerate(
             (
                 (dest_hbm, dest),
@@ -158,8 +159,9 @@
         for z in (0, LEVELS + 1):
             start[f, z, 8:40] = zero
             first[f, z, 8:40] = zero
-    for load in loads[3:7]:
-        load.wait()
+    loads[3].wait()
+    upper = outgoing.at[pl.ds(0, 3), pl.ds(0, 360)]
+    pltpu.make_async_copy(upper, upper, load_sem.at[4]).wait()
     twice = cost[...].astype(jnp.float32) >= 2.0
 
     chosen_pair = jnp.concatenate([chosen, chosen], axis=1)
@@ -263,8 +265,9 @@
         along = (index // 16 % 2) * 3 + index % 4
         return across * 8 + along
 
-    pltpu.make_async_copy(faces, faces, face_send).wait()
-    pltpu.make_async_copy(halo, halo, face_recv).wait()
+    moved_rows = pl.ds(0, 52)
+    pltpu.make_async_copy(faces.at[moved_rows], faces.at[moved_rows], face_send).wait()
+    pltpu.make_async_copy(halo.at[moved_rows], halo.at[moved_rows], face_recv).wait()
     shared = jnp.where(place(row) == place(lane), 1.0, 0.0)
     hside = jnp.where(hrow < 8, 96, 0) + (hrow % 8 // 4) * 3 + hrow % 4
     hfront = ((hrow % 16 // 4) * 3 + hrow % 4) * 8 + jnp.where(hrow < 32, 6, 0)
@@ -275,7 +278,8 @@
     hplace = jnp.where(hrow < 16, hside, jnp.where(hrow < 48, hfront, hcorner))
     met = jnp.where(hplace == place(hlane), 1.0, 0.0)
     summed = jnp.dot(weighted[...], shared, precision=HIGHEST, preferred_element_type=jnp.float32)
-    summed = summed + tn_dot(halo[...], met, HIGHEST)
+    arrived = jnp.where((hrow < 48) | (hrow % 8 == 0), halo[...], 0.0)
+    summed = summed + tn_dot(arrived, met, HIGHEST)
     below = summed[60:72]
     for f in range(FIELDS):
         gcm_new[f] = jnp.swapaxes(summed[f * LEVELS:(f + 1) * LEVELS] / below, 0, 1)
@@ -330,7 +334,7 @@
             pltpu.VMEM((OWNED, LEVELS), jnp.float32),
             pltpu.VMEM((1, OWNED), jnp.int32),
             pltpu.VMEM((1, OWNED), jnp.int32),
-            pltpu.SemaphoreType.DMA((8,)),
+            pltpu.SemaphoreType.DMA((6,)),
             pltpu.SemaphoreType.REGULAR((2,)),
             pltpu.SemaphoreType.DMA,
             pltpu.SemaphoreType.DMA,

time: 35.3 us -> 35.2 us (level); the launches traced: 35.2 us -> 34.6 us
  Pallas kernels: 34.5 us -> 34 us
    pallas_call x1, Pallas kernels: 33 us -> 32.5 us  [body(): pl.pallas_call(cloud_kernel, out_shape=(jax.ShapeDtypeStruct((BLOCKS, BLO...]
where the time goes in v6:
time: 35.2 us; the launch traced here: 34.6 us
  Pallas kernels  34 us (97%)
  between operations  0.64 us (2%)
    pallas_call x1, Pallas kernels, body(): pl.pallas_call(cloud_kernel, out_shape=(jax.ShapeDtypeStruct((BLOCKS, BLO...  32.5 us
    pallas_call x1, Pallas kernels, body(): pl.pallas_call(unpack_kernel, out_shape=(jax.ShapeDtypeStruct((FIELDS, LE...  1.48 us

profile of v6, /device:TPU:1, one launch (start us, length us, event | category | flops | bytes accessed | tf_op | source)
XLA Modules:
  0.0 34.6 jit_solution(7676466639872386274)
XLA Ops:
  0.6 32.5 %clouds.1 = (f32[6,640,128]{2,1,0:T(8,128)S(1)}, f32[5,128,12]{2,1,0:T(8,128)S(1)}) custom-call(f32[5,12,32,128]{3,2,1,0:T(8,128)} %crm.1, f32[5,128,12]{2,1,0:T(8,128)} %bitcast.12, f32[128,12]{1,0:T(8,128)} %bitcast.13, s32[1,128]{1,0:T(1,128)} %bitcast.14, s32[1,128]{1,0:T(1,128)} %bitcast.15), custom_call_target="tpu_custom_call" | custom-call | tf_op jit(solution)/shard_map/clouds/pallas_call | solution.py:314
  33.2 1.5 %unpack.1 = (f32[5,384,256]{2,1,0:T(8,128)}, f32[5,128,12]{2,1,0:T(8,128)}) custom-call(f32[6,640,128]{2,1,0:T(8,128)S(1)} %get-tuple-element.6.landed, f32[5,128,12]{2,1,0:T(8,128)S(1)} %get-tuple-element.7.gcm_in), custom_call_target="tpu_custom_call" | custom-call | tf_op jit(solution)/shard_map/unpack/pallas_call | solution.py:350
